TPU v7x, 32 devices: a whole 2x2x4 slice. The times are simulated.
32 devices in a mesh: grp: 2 (over y), ctx: 4 (over z), tp: 2 (over x), sub: 2 (over core).
Axes of the slice: x: 2, y: 2, z: 4, core: 2. Of those that a mesh axis runs over, the one named last changes fastest.
Arguments:
- context: bfloat16 [3072, 2048], P(('grp', 'ctx'), ('tp', 'sub')), parts along dimension 0, may hold values from -24 to 24
- context_pos: int32 [3072], P(('grp', 'ctx')), parts along dimension 0, may hold values from 0 to 1535, each once
- latent_in: bfloat16 [64, 2048], P(('grp', 'ctx')), parts along dimension 0, may hold values from -24 to 24
- latent_start: int32 [2], P('grp'), parts along dimension 0, may hold values from 768 to 1504
- ctx_gain: float32 [2048], replicated, may hold values from 0.25 to 1.75
- lat_gain: float32 [2048], replicated, may hold values from 0.25 to 1.75
- mid_gain: float32 [2048], replicated, may hold values from 0.25 to 1.75
- cross_q: bfloat16 [2048, 2048], P('ctx', ('tp', 'sub')), may hold values from -2 to 2
- cross_k: bfloat16 [2048, 2048], P('ctx', ('tp', 'sub')), may hold values from -2 to 2
- cross_v: bfloat16 [2048, 2048], P('ctx', ('tp', 'sub')), may hold values from -0.125 to 0.125
- cross_out: bfloat16 [2048, 2048], P('ctx', ('tp', 'sub')), may hold values from -0.125 to 0.125
- self_qkv: bfloat16 [2048, 3, 2048], P('ctx', None, ('tp', 'sub')), may hold values from -2 to 2
- self_out: bfloat16 [2048, 2048], P('ctx', ('tp', 'sub')), may hold values from -0.125 to 0.125
Outputs:
- latent_out: bfloat16 [64, 2048], P(('grp', 'ctx'), ('tp', 'sub')), parts along dimension 0
There are 2 independent parts, one for each index of `grp`. A program takes and returns all parts, laid end to end along the dimension named above; an argument that names none is the same for every part. Nothing has to cross between parts.
Inputs may be any that keep to these rules, and one draw needn't show every extreme that they name: context_pos holds each of 0 to 1535 once.
All inputs are finite; a program needn't handle non-finite values.
Results may differ from a plain program's by a relative error of at most 0.035.
Values may be sent and summed in bfloat16 or wider, within the bound.
A program may use at most 64 MiB of HBM per device.

v0:
```python
import math
import jax
import jax.numpy as jnp
from jax import lax
from jax.sharding import PartitionSpec as P

DH = 128
EPS = 1e-05
NEG = -1e30


def combined_all(shard, axis, combine):
    everything = jax.tree.map(
        lambda part, kind: lax.all_gather(part.astype(kind), axis),
        shard,
        (jnp.bfloat16, jnp.bfloat16, jnp.bfloat16),
    )

    def take(k):
        return jax.tree.map(lambda part, own: part[k].astype(own.dtype), everything, shard)

    return lax.fori_loop(
        1, lax.axis_size(axis), lambda k, so_far: combine(so_far, take(k)), take(0)
    )


def rms_rows(values, gain):
    wide = values.astype(jnp.float32)
    scale = lax.rsqrt(jnp.mean(wide * wide, axis=-1, keepdims=True) + EPS)
    return (wide * scale * gain).astype(jnp.bfloat16)


def contract_last(left, right):
    return lax.dot_general(
        left, right, (((1,), (1,)), ((), ())), preferred_element_type=jnp.float32
    )


def softmax_parts(queries, keys, values, allowed):
    heads = queries.shape[1] // DH
    maxima = []
    totals = []
    numerators = []
    for head in range(heads):
        begin = head * DH
        scores = contract_last(queries[:, begin : begin + DH], keys[:, begin : begin + DH]) * (
            1.0 / math.sqrt(DH)
        )
        scores = jnp.where(allowed, scores, NEG)
        top = jnp.max(scores, axis=1)
        weights = jnp.where(allowed, jnp.exp(scores - top[:, None]), 0.0)
        maxima.append(top)
        totals.append(jnp.sum(weights, axis=1))
        numerators.append(
            jnp.dot(
                weights.astype(jnp.bfloat16),
                values[:, begin : begin + DH],
                preferred_element_type=jnp.float32,
            )
        )
    return (
        jnp.stack(maxima, axis=1),
        jnp.stack(totals, axis=1),
        jnp.concatenate(numerators, axis=1),
    )


def combine_parts(first, second):
    top = jnp.maximum(first[0], second[0])
    first_factor = jnp.exp(first[0] - top)
    second_factor = jnp.exp(second[0] - top)
    totals = first[1] * first_factor + second[1] * second_factor
    numerators = first[2] * jnp.repeat(first_factor, DH, axis=1) + second[2] * jnp.repeat(
        second_factor, DH, axis=1
    )
    return (top, totals, numerators)


def on_device(
    context,
    context_pos,
    latent_in,
    latent_start,
    ctx_gain,
    lat_gain,
    mid_gain,
    cross_q,
    cross_k,
    cross_v,
    cross_out,
    self_qkv,
    self_out,
):
    owned = latent_in.shape[0]
    columns = cross_q.shape[1]
    whole = lax.all_gather(context, ("tp", "sub"), axis=1, tiled=True)
    normed_ctx = rms_rows(whole, ctx_gain)
    normed_lat = rms_rows(latent_in, lat_gain)
    query_sum = jnp.dot(
        normed_lat,
        lax.all_gather(cross_q, "ctx", axis=0, tiled=True),
        preferred_element_type=jnp.float32,
    )
    key_sum = jnp.dot(
        normed_ctx,
        lax.all_gather(cross_k, "ctx", axis=0, tiled=True),
        preferred_element_type=jnp.float32,
    )
    value_sum = jnp.dot(
        normed_ctx,
        lax.all_gather(cross_v, "ctx", axis=0, tiled=True),
        preferred_element_type=jnp.float32,
    )
    keys = key_sum.astype(jnp.bfloat16)
    values = value_sum.astype(jnp.bfloat16)
    queries = lax.all_gather(query_sum.astype(jnp.bfloat16), "ctx", axis=0, tiled=True)
    query_pos = latent_start[0] + jnp.arange(queries.shape[0], dtype=jnp.int32)
    allowed = context_pos[None, :] <= query_pos[:, None]
    maxima, totals, numerators = softmax_parts(queries, keys, values, allowed)
    first_row = lax.axis_index("ctx") * owned
    maxima, totals, numerators = combined_all((maxima, totals, numerators), "ctx", combine_parts)
    totals = lax.dynamic_slice_in_dim(totals, first_row, owned, 0)
    numerators = lax.dynamic_slice_in_dim(numerators, first_row, owned, 0)
    attended = (numerators / jnp.repeat(totals, DH, axis=1)).astype(jnp.bfloat16)
    cross_terms = contract_last(attended, lax.all_gather(cross_out, "ctx", axis=0, tiled=True))
    cross_sum = lax.psum(cross_terms.astype(jnp.bfloat16), ("tp", "sub")).astype(jnp.float32)
    hidden = (latent_in.astype(jnp.float32) + cross_sum).astype(jnp.bfloat16)
    normed_mid = rms_rows(hidden, mid_gain)
    piece = lax.all_gather(self_qkv, "ctx", axis=0, tiled=True)
    span = piece.shape[0]
    projected = jnp.dot(
        normed_mid, piece.reshape(span, 3 * columns), preferred_element_type=jnp.float32
    )
    projected = projected.astype(jnp.bfloat16).reshape(owned, 3, columns)
    gathered = lax.all_gather(projected[:, 1:], "ctx", axis=0, tiled=True)
    key_index = jnp.arange(gathered.shape[0], dtype=jnp.int32)
    row_index = first_row + jnp.arange(owned, dtype=jnp.int32)
    causal = key_index[None, :] <= row_index[:, None]
    unused, self_totals, self_numerators = softmax_parts(
        projected[:, 0], gathered[:, 0], gathered[:, 1], causal
    )
    attended_self = (self_numerators / jnp.repeat(self_totals, DH, axis=1)).astype(jnp.bfloat16)
    self_terms = contract_last(attended_self, lax.all_gather(self_out, "ctx", axis=0, tiled=True))
    summed = lax.psum_scatter(
        self_terms.astype(jnp.bfloat16), ("tp", "sub"), scatter_dimension=1, tiled=True
    ).astype(jnp.float32)
    share = summed.shape[1]
    residual = lax.dynamic_slice_in_dim(hidden, lax.axis_index(("tp", "sub")) * share, share, 1)
    return (residual.astype(jnp.float32) + summed).astype(jnp.bfloat16)


def solution(mesh):
    return jax.shard_map(
        on_device,
        mesh=mesh,
        in_specs=(
            P(("grp", "ctx"), ("tp", "sub")),
            P(("grp", "ctx")),
            P(("grp", "ctx"), None),
            P("grp"),
            P(),
            P(),
            P(),
            P("ctx", ("tp", "sub")),
            P("ctx", ("tp", "sub")),
            P("ctx", ("tp", "sub")),
            P("ctx", ("tp", "sub")),
            P("ctx", None, ("tp", "sub")),
            P("ctx", ("tp", "sub")),
        ),
        out_specs=P(("grp", "ctx"), ("tp", "sub")),
        check_vma=False,
    )
```

profile of v0, /device:TPU:0, one launch (start us, length us, event | category | flops | bytes accessed | tf_op | source)
XLA Modules:
  0.0 410.3 jit_solution(3761533873180696968)
XLA Ops:
  6.5 0.7 all-gather.10.cloned.1.call-update
  7.3 0.7 all-gather.8.cloned.1.call-update
  8.1 0.7 all-gather.12.cloned.1.call-update
  8.8 0.5 all-gather.14.cloned.1.call-update
  9.4 0.5 all-gather.16.cloned.1.call-update
  10.0 1.6 copy.21
  11.6 0.0 all-gather.20.cloned.1.call-start
  11.7 0.7 all-gather.20.cloned.1.call-update
  13.1 0.1 fusion.31
  13.2 18.1 %all-gather.10.cloned.1.call-done = bf16[384,2048]{1,0:T(8,128)(2,1)} async-done(((bf16[384,512]{1,0:T(8,128)(2,1)}), bf16[384,2048]{1,0:T(8,128)(2,1)}) %all-gather.10.cloned.1.call-update) | async-done | bytes 1572880 | tf_op jit(solution)/shard_map/all_gather | solution.py:96
  31.3 1.9 fusion.3
  33.2 45.6 %all-gather.8.cloned.1.call-done = bf16[2048,512]{1,0:T(8,128)(2,1)} async-done(((bf16[512,512]{1,0:T(8,128)(2,1)}), bf16[2048,512]{1,0:T(8,128)(2,1)}) %all-gather.8.cloned.1.call-update) | async-done | bytes 2097168 | tf_op jit(solution)/shard_map/all_gather | solution.py:101
  78.9 2.0 convolution_convert_fusion.9
  80.9 13.3 %all_gather.40 = bf16[32,512]{1,0:T(8,128)(2,1)S(1)} all-gather(bf16[8,512]{1,0:T(8,128)(2,1)S(1)} %convolution_convert_fusion.9), channel_id=1, replica_groups=mesh['grp'=2,'ctx'=4,'tp'=2,'sub'=2] {'ctx'}, dimensions={0}, use_global_device_ids=true | all-gather | bytes 40960 | tf_op jit(solution)/shard_map/all_gather | solution.py:116
  94.2 31.1 %all-gather.12.cloned.1.call-done = bf16[2048,512]{1,0:T(8,128)(2,1)} async-done(((bf16[512,512]{1,0:T(8,128)(2,1)}), bf16[2048,512]{1,0:T(8,128)(2,1)}) %all-gather.12.cloned.1.call-update) | async-done | bytes 2097168 | tf_op jit(solution)/shard_map/all_gather | solution.py:106
  125.3 2.6 convolution_convert_fusion.4
  127.9 0.3 fusion.137
  128.2 0.3 fusion.136
  128.4 0.3 fusion.135
  128.7 0.3 fusion.134
  129.0 42.7 %all-gather.14.cloned.1.call-done = bf16[2048,512]{1,0:T(8,128)(2,1)} async-done(((bf16[512,512]{1,0:T(8,128)(2,1)}), bf16[2048,512]{1,0:T(8,128)(2,1)}) %all-gather.14.cloned.1.call-update) | async-done | bytes 2097168 | tf_op jit(solution)/shard_map/all_gather | solution.py:111
  171.7 2.6 convolution_convert_fusion.3
  174.3 0.2 fusion.10
  174.5 0.2 fusion.11
  174.7 0.2 fusion.12
  174.9 0.2 fusion.13
  175.1 0.2 fusion.36
  175.4 14.4 %all_gather.46 = bf16[4,32,512]{2,1,0:T(8,128)(2,1)S(1)} all-gather(bf16[1,32,512]{2,1,0:T(8,128)(2,1)S(1)} %pad_maximum_fusion), channel_id=1, replica_groups=mesh['grp'=2,'ctx'=4,'tp'=2,'sub'=2] {'ctx'}, dimensions={0}, use_global_device_ids=true | all-gather | bytes 163840 | tf_op jit(solution)/shard_map/all_gather | solution.py:14
  189.9 8.6 %all_gather.44 = bf16[4,32,4]{1,2,0:T(4,128)(2,1)S(1)} all-gather(bf16[1,32,4]{1,2,0:T(4,128)(2,1)S(1)} %pad_maximum_fusion.3), channel_id=1, replica_groups=mesh['grp'=2,'ctx'=4,'tp'=2,'sub'=2] {'ctx'}, dimensions={0}, use_global_device_ids=true | all-gather | bytes 1280 | tf_op jit(solution)/shard_map/all_gather | solution.py:14
  198.5 9.3 %all_gather.43 = bf16[4,32,4]{1,2,0:T(4,128)(2,1)S(1)} all-gather(bf16[1,32,4]{1,2,0:T(4,128)(2,1)S(1)} %pad_maximum_fusion.2), channel_id=1, replica_groups=mesh['grp'=2,'ctx'=4,'tp'=2,'sub'=2] {'ctx'}, dimensions={0}, use_global_device_ids=true | all-gather | bytes 1280 | tf_op jit(solution)/shard_map/all_gather | solution.py:14
  207.8 1.3 while.19
  207.8 0.1 copy.32
  207.9 0.1 broadcast_in_dim.134
  208.0 0.1 copy.33
  208.1 0.1 broadcast_in_dim.135
  208.3 0.1 copy.32
  208.4 0.1 broadcast_in_dim.134
  208.4 0.1 copy.33
  208.5 0.1 broadcast_in_dim.135
  208.7 0.1 copy.32
  208.8 0.1 broadcast_in_dim.134
  208.9 0.1 copy.33
  209.0 0.1 broadcast_in_dim.135
  209.1 0.1 constant_dynamic-slice_fusion.1
  209.2 9.8 %all-gather.16.cloned.1.call-done = bf16[2048,512]{1,0:T(8,128)(2,1)} async-done(((bf16[512,512]{1,0:T(8,128)(2,1)}), bf16[2048,512]{1,0:T(8,128)(2,1)}) %all-gather.16.cloned.1.call-update) | async-done | bytes 2097168 | tf_op jit(solution)/shard_map/all_gather | solution.py:125
  219.0 2.2 convolution_convert_fusion.2
  221.3 11.4 %psum.7 = bf16[8,2048]{1,0:T(8,128)(2,1)S(1)} all-reduce(bf16[8,2048]{1,0:T(8,128)(2,1)S(1)} %convolution_convert_fusion.2), channel_id=1, replica_groups=mesh['grp'=2,'ctx'=4,'tp'=2,'sub'=2] {'tp','sub'}, use_global_device_ids=true, to_apply=%region_12.13 | all-reduce | flops 16384 | bytes 65536 | tf_op jit(solution)/shard_map/psum | solution.py:126
  232.7 0.1 fusion.28
  232.8 101.9 %all-gather.18.cloned.1.call-done = bf16[2048,3,512]{0,2,1:T(8,128)(2,1)} async-done(((bf16[512,3,512]{0,2,1:T(8,128)(2,1)}), bf16[2048,3,512]{0,2,1:T(8,128)(2,1)}) %all-gather.18.cloned.1.call-update) | async-done | bytes 6291472 | tf_op jit(solution)/shard_map/all_gather | solution.py:129
  334.8 4.5 %convolution_convert_fusion.1 = bf16[8,1536]{1,0:T(8,128)(2,1)S(1)} fusion(bf16[2048,1536]{0,1:T(8,128)(2,1)} %bitcast.107, bf16[8,2048]{1,0:T(8,128)(2,1)S(1)} %get-tuple-element.211, f32[2048]{0:T(1024)S(1)} %copy-done.4, f32[8]{0:T(128)S(1)} %add_rsqrt_fusion.1), kind=kOutput, calls=%fused_computation.16 | convolution fusion | flops 50409472 | bytes 6357024 | tf_op jit(solution)/shard_map/dot_general | solution.py:131
  339.3 13.6 %all_gather.49 = bf16[32,2,512]{2,0,1:T(8,128)(2,1)S(1)} all-gather(bf16[8,2,512]{2,0,1:T(8,128)(2,1)S(1)} %slice.141), channel_id=1, replica_groups=mesh['grp'=2,'ctx'=4,'tp'=2,'sub'=2] {'ctx'}, dimensions={0}, use_global_device_ids=true | all-gather | bytes 81920 | tf_op jit(solution)/shard_map/all_gather | solution.py:135
  352.9 0.2 fusion.141
  353.1 0.2 fusion.140
  353.3 0.2 fusion.139
  353.6 0.2 fusion.138
  353.8 0.2 fusion.92
  354.1 0.2 fusion.83
  354.3 0.2 fusion.80
  354.4 0.2 fusion.77
  354.6 0.2 fusion.74
  354.8 26.4 %all-gather.20.cloned.1.call-done = bf16[2048,512]{1,0:T(8,128)(2,1)} async-done(((bf16[512,512]{1,0:T(8,128)(2,1)}), bf16[2048,512]{1,0:T(8,128)(2,1)}) %all-gather.20.cloned.1.call-update) | async-done | bytes 2097168 | tf_op jit(solution)/shard_map/all_gather | solution.py:143
  381.2 2.9 convolution_convert_fusion
  384.1 18.1 %reduce-scatter.2.cloned.1.call-done = bf16[8,512]{1,0:T(8,128)(2,1)} async-done(((bf16[8,2048]{1,0:T(8,128)(2,1)}), bf16[8,512]{1,0:T(8,128)(2,1)}) %reduce-scatter.2.cloned.1.call-update) | async-done | bytes 8208 | tf_op jit(solution)/shard_map/reduce_scatter | solution.py:144
  402.2 1.3 add_convert_fusion
  (46 shorter events, 0.6 us)
Async XLA Ops:
  6.5 3.4 copy-start
  6.5 24.8 %all-gather.10.cloned.1.call-start = ((), (), s32[]{:S(2)}) async-start(), calls=%async_computation.2 | async-start | bytes 1966080 | tf_op jit(solution)/shard_map/all_gather | solution.py:96
  7.3 71.6 %all-gather.8.cloned.1.call-start = ((), (), s32[]{:S(2)}) async-start(), calls=%async_computation.1 | async-start | bytes 2621440 | tf_op jit(solution)/shard_map/all_gather | solution.py:101
  8.0 117.3 %all-gather.12.cloned.1.call-start = ((), (), s32[]{:S(2)}) async-start(), calls=%async_computation.3 | async-start | bytes 2621440 | tf_op jit(solution)/shard_map/all_gather | solution.py:106
  8.7 162.9 %all-gather.14.cloned.1.call-start = ((), (), s32[]{:S(2)}) async-start(), calls=%async_computation.4 | async-start | bytes 2621440 | tf_op jit(solution)/shard_map/all_gather | solution.py:111
  9.3 209.7 %all-gather.16.cloned.1.call-start = ((), (), s32[]{:S(2)}) async-start(), calls=%async_computation.5 | async-start | bytes 2621440 | tf_op jit(solution)/shard_map/all_gather | solution.py:125
  9.9 3.2 copy-start.2
  9.9 324.8 %all-gather.18.cloned.1.call-start = ((), (), s32[]{:S(2)}) async-start(), calls=%async_computation.6 | async-start | bytes 7864320 | tf_op jit(solution)/shard_map/all_gather | solution.py:129
  11.6 67.3 %copy-start.3 = (f32[2048]{0:T(1024)S(1)}, f32[2048]{0:T(1024)}, u32[]{:S(2)}) copy-start(f32[2048]{0:T(1024)} %param.20) | copy-start | bytes 24580
  11.6 113.7 %copy-start.6 = (f32[2048]{0:T(1024)S(1)}, f32[2048]{0:T(1024)}, u32[]{:S(2)}) copy-start(f32[2048]{0:T(1024)} %param.19) | copy-start | bytes 24580
  11.6 369.6 %all-gather.20.cloned.1.call-start = ((), (), s32[]{:S(2)}) async-start(), calls=%async_computation.7 | async-start | bytes 2621440 | tf_op jit(solution)/shard_map/all_gather | solution.py:143
  12.4 389.8 %reduce-scatter.2.cloned.1.call-start = ((), (), s32[]{:S(2)}) async-start(), calls=%async_computation.8 | async-start | bytes 40960 | tf_op jit(solution)/shard_map/reduce_scatter | solution.py:144
  31.3 94.0 %copy-start.1 = (bf16[384,2048]{1,0:T(8,128)(2,1)S(1)}, bf16[384,2048]{1,0:T(8,128)(2,1)}, u32[]{:S(2)}) copy-start(bf16[384,2048]{1,0:T(8,128)(2,1)} %all-gather.10.cloned.1.call-done) | copy-start | bytes 4718596
  94.2 33.7 %copy-start.5 = (s32[384]{0:T(512)S(1)}, s32[384]{0:T(512)}, u32[]{:S(2)}) copy-start(s32[384]{0:T(512)} %param.16) | copy-start | bytes 4612
  207.8 127.0 %copy-start.4 = (f32[2048]{0:T(1024)S(1)}, f32[2048]{0:T(1024)}, u32[]{:S(2)}) copy-start(f32[2048]{0:T(1024)} %param.21) | copy-start | bytes 24580
Sparse Core Ops, SparseCore 0:
  8.9 22.3 all-gather.9
  32.9 45.9 all-gather.7
  80.4 44.7 all-gather.11
  126.7 44.9 all-gather.13
  173.1 45.9 all-gather.15
  220.5 114.2 all-gather.17
  336.3 44.8 all-gather.19
  384.2 17.9 reduce-scatter.1
where the time goes:
time: 411 us; the launch traced here: 410 us
  waiting for transfers between devices  298 us (73%)
  blocking collectives  70.6 us (17%)
  matrix products  20.4 us (5%)
  between operations  14.3 us (3%)
  other arithmetic  4.19 us (1%)
    all_gather x1, waiting for transfers between devices, on_device(): piece = lax.all_gather(self_qkv, 'ctx', axis=0, tiled=True)  102 us
    all_gather x1, waiting for transfers between devices, on_device(): lax.all_gather(cross_q, 'ctx', axis=0, tiled=True)  45.6 us
    all_gather x1, waiting for transfers between devices, on_device(): lax.all_gather(cross_v, 'ctx', axis=0, tiled=True)  42.7 us
    all_gather x3, blocking collectives, combined_all(): lax.all_gather(part.astype(kind), axis)  32.3 us
    all_gather x1, waiting for transfers between devices, on_device(): lax.all_gather(cross_k, 'ctx', axis=0, tiled=True)  31.1 us
    all_gather x1, waiting for transfers between devices, on_device(): lax.all_gather(self_out, 'ctx', axis=0, tiled=True)  26.4 us
    reduce_scatter x1, waiting for transfers between devices, on_device(): lax.psum_scatter(self_terms.astype(jnp.bfloat16), ('tp', 'sub'), scatter_...  18.1 us
    all_gather x1, waiting for transfers between devices, on_device(): whole = lax.all_gather(context, ('tp', 'sub'), axis=1, tiled=True)  18.1 us
  transfers between devices with their start and end apart: 8, of which 8 were waited for; matrix products, arithmetic and copies ran while one was open for 6% of the time, Pallas kernels for 0%

commit v1 on v0

--- a/solution.py
+++ b/solution.py
@@ -7,6 +7,28 @@
 DH = 128
 EPS = 1e-05
 NEG = -1e30
+
+
+def in_order(blocks, dim):
+    shape = list(blocks.shape[1:])
+    shape[dim] *= blocks.shape[0]
+    return jnp.moveaxis(blocks, 0, dim).reshape(shape)
+
+
+def ring_gather(x, axis, dim):
+    size = lax.axis_size(axis)
+    pairs = [(i, (i + 1) % size) for i in range(size)]
+    back = [(b, a) for a, b in pairs]
+    lower, upper = ([], [])
+    for step in range(size - 1):
+        if step % 2 == 0:
+            lower.append(lax.ppermute(lower[-1] if lower else x, axis, pairs))
+        else:
+            upper.append(lax.ppermute(upper[-1] if upper else x, axis, back))
+    tiles = jnp.stack([*lower[::-1], x, *upper])
+    shift = lax.axis_index(axis) - len(lower)
+    tiles = tiles[(jnp.arange(size) - shift) % size]
+    return in_order(tiles, dim)
 
 
 def combined_all(shard, axis, combine):
@@ -97,9 +119,7 @@
     normed_ctx = rms_rows(whole, ctx_gain)
     normed_lat = rms_rows(latent_in, lat_gain)
     query_sum = jnp.dot(
-        normed_lat,
-        lax.all_gather(cross_q, "ctx", axis=0, tiled=True),
-        preferred_element_type=jnp.float32,
+        normed_lat, ring_gather(cross_q, "ctx", 0), preferred_element_type=jnp.float32
     )
     key_sum = jnp.dot(
         normed_ctx,

time: 411 us -> 371 us (0.903)
  waiting for transfers between devices: 298 us -> 239 us
  blocking collectives: 70.6 us -> 80.1 us
  starting transfers between devices: 0.27 us -> 5.41 us
    all_gather x1 -> x0, waiting for transfers between devices: 45.6 us -> none  [on_device(): lax.all_gather(cross_q, 'ctx', axis=0, tiled=True)]
    ppermute x0 -> x3, waiting for transfers between devices: none -> 41.2 us  [the longest x2 31.4 us: ring_gather(): lower.append(lax.ppermute(lower[-1] if lower else x, axis, pairs))]
    all_gather x1, waiting for transfers between devices: 31.1 us -> 0.02 us  [on_device(): lax.all_gather(cross_k, 'ctx', axis=0, tiled=True)]
    all_gather x1, waiting for transfers between devices: 18.1 us -> 0.01 us  [on_device(): whole = lax.all_gather(context, ('tp', 'sub'), axis=1, tiled=True)]
    all_gather x1, blocking collectives: 13.3 us -> 22.8 us  [on_device(): lax.all_gather(query_sum.astype(jnp.bfloat16), 'ctx', axis=0, tiled=True)]
    ppermute x0 -> x3, starting transfers between devices: none -> 5.17 us  [the longest x2 3.08 us: ring_gather(): lower.append(lax.ppermute(lower[-1] if lower else x, axis, pairs))]
  transfers between devices with their start and end apart: 8 -> 10, of which waited for: 8 -> 8; matrix products, arithmetic and copies ran while one was open for 6% -> 7% of each run, Pallas kernels for 0% -> 0%
where the time goes in v1:
time: 371 us
  waiting for transfers between devices  239 us (64%)
  blocking collectives  80.1 us (22%)
  matrix products  21 us (6%)
  between operations  14.4 us (4%)
  starting transfers between devices  5.41 us (1%)
  other arithmetic  5.4 us (1%)
  local copies, waits for them, and re-layouts  4.8 us (1%)
    all_gather x1, waiting for transfers between devices, on_device(): piece = lax.all_gather(self_qkv, 'ctx', axis=0, tiled=True)  102 us
    all_gather x1, waiting for transfers between devices, on_device(): lax.all_gather(cross_v, 'ctx', axis=0, tiled=True)  39.4 us
    all_gather x3, blocking collectives, combined_all(): lax.all_gather(part.astype(kind), axis)  32.3 us
    ppermute x2, waiting for transfers between devices, ring_gather(): lower.append(lax.ppermute(lower[-1] if lower else x, axis, pairs))  31.4 us
    all_gather x1, waiting for transfers between devices, on_device(): lax.all_gather(self_out, 'ctx', axis=0, tiled=True)  26.1 us
    all_gather x1, blocking collectives, on_device(): lax.all_gather(query_sum.astype(jnp.bfloat16), 'ctx', axis=0, tiled=True)  22.8 us
    reduce_scatter x1, waiting for transfers between devices, on_device(): lax.psum_scatter(self_terms.astype(jnp.bfloat16), ('tp', 'sub'), scatter_...  18.3 us
    all_gather x1, blocking collectives, on_device(): gathered = lax.all_gather(projected[:, 1:], 'ctx', axis=0, tiled=True)  13.6 us
  transfers between devices with their start and end apart: 10, of which 8 were waited for; matrix products, arithmetic and copies ran while one was open for 7% of the time, Pallas kernels for 0%

profile of v1, /device:TPU:0, one launch (start us, length us, event | category | flops | bytes accessed | tf_op | source)
XLA Modules:
  0.0 370.6 jit_solution(16252477635154419502)
XLA Ops:
  6.5 0.7 all-gather.7.cloned.1.call-update
  7.3 0.7 all-gather.9.cloned.1.call-update
  8.1 0.7 all-gather.11.cloned.1.call-update
  8.8 0.5 all-gather.13.cloned.1.call-update
  9.4 1.6 copy.21
  11.1 3.1 collective-permute-start
  14.1 2.1 collective-permute-start.2
  17.0 12.0 %collective-permute-done = bf16[512,512]{1,0:T(8,128)(2,1)S(1)} collective-permute-done((bf16[512,512]{1,0:T(8,128)(2,1)S(1)}, bf16[512,512]{1,0:T(8,128)(2,1)S(1)}, u32[]{:S(2)}, u32[]{:S(2)}) %collective-permute-start) | collective-permute-done | bytes 524320 | tf_op jit(solution)/shard_map/ppermute | solution.py:25
  29.0 0.1 fusion.31
  29.1 9.9 %collective-permute-done.2 = bf16[512,512]{1,0:T(8,128)(2,1)S(1)} collective-permute-done((bf16[512,512]{1,0:T(8,128)(2,1)S(1)}, bf16[512,512]{1,0:T(8,128)(2,1)S(1)}, u32[]{:S(2)}, u32[]{:S(2)}) %collective-permute-start.2) | collective-permute-done | bytes 524320 | tf_op jit(solution)/shard_map/ppermute | solution.py:27
  39.0 19.4 %collective-permute-done.1 = bf16[512,512]{1,0:T(8,128)(2,1)S(1)} collective-permute-done((bf16[512,512]{1,0:T(8,128)(2,1)S(1)}, bf16[512,512]{1,0:T(8,128)(2,1)S(1)}, u32[]{:S(2)}, u32[]{:S(2)}) %collective-permute-start.1) | collective-permute-done | bytes 524320 | tf_op jit(solution)/shard_map/ppermute | solution.py:25
  58.4 1.3 pad_maximum_fusion
  59.7 2.0 gather_fusion
  61.7 2.0 convolution_convert_fusion.9
  63.8 22.8 %all_gather.36 = bf16[32,512]{1,0:T(8,128)(2,1)S(1)} all-gather(bf16[8,512]{1,0:T(8,128)(2,1)S(1)} %convolution_convert_fusion.9), channel_id=1, replica_groups=mesh['grp'=2,'ctx'=4,'tp'=2,'sub'=2] {'ctx'}, dimensions={0}, use_global_device_ids=true | all-gather | bytes 40960 | tf_op jit(solution)/shard_map/all_gather | solution.py:136
  86.6 1.8 fusion.3
  88.4 3.2 convolution_convert_fusion.4
  91.6 0.3 fusion.139
  91.9 0.3 fusion.138
  92.2 0.3 fusion.137
  92.4 0.3 fusion.136
  92.7 39.4 %all-gather.11.cloned.1.call-done = bf16[2048,512]{1,0:T(8,128)(2,1)} async-done(((bf16[512,512]{1,0:T(8,128)(2,1)}), bf16[2048,512]{1,0:T(8,128)(2,1)}) %all-gather.11.cloned.1.call-update) | async-done | bytes 2097168 | tf_op jit(solution)/shard_map/all_gather | solution.py:131
  132.1 2.6 convolution_convert_fusion.3
  134.7 0.2 fusion.10
  134.9 0.2 fusion.11
  135.1 0.2 fusion.12
  135.3 0.2 fusion.13
  135.5 0.2 fusion.36
  135.8 14.4 %all_gather.42 = bf16[4,32,512]{2,1,0:T(8,128)(2,1)S(1)} all-gather(bf16[1,32,512]{2,1,0:T(8,128)(2,1)S(1)} %pad_maximum_fusion.1), channel_id=1, replica_groups=mesh['grp'=2,'ctx'=4,'tp'=2,'sub'=2] {'ctx'}, dimensions={0}, use_global_device_ids=true | all-gather | bytes 163840 | tf_op jit(solution)/shard_map/all_gather | solution.py:36
  150.3 8.6 %all_gather.40 = bf16[4,32,4]{1,2,0:T(4,128)(2,1)S(1)} all-gather(bf16[1,32,4]{1,2,0:T(4,128)(2,1)S(1)} %pad_maximum_fusion.4), channel_id=1, replica_groups=mesh['grp'=2,'ctx'=4,'tp'=2,'sub'=2] {'ctx'}, dimensions={0}, use_global_device_ids=true | all-gather | bytes 1280 | tf_op jit(solution)/shard_map/all_gather | solution.py:36
  158.9 9.3 %all_gather.39 = bf16[4,32,4]{1,2,0:T(4,128)(2,1)S(1)} all-gather(bf16[1,32,4]{1,2,0:T(4,128)(2,1)S(1)} %pad_maximum_fusion.3), channel_id=1, replica_groups=mesh['grp'=2,'ctx'=4,'tp'=2,'sub'=2] {'ctx'}, dimensions={0}, use_global_device_ids=true | all-gather | bytes 1280 | tf_op jit(solution)/shard_map/all_gather | solution.py:36
  168.2 1.3 while.19
  168.2 0.1 copy.32
  168.3 0.1 broadcast_in_dim.135
  168.4 0.1 copy.33
  168.5 0.1 broadcast_in_dim.136
  168.7 0.1 copy.32
  168.8 0.1 broadcast_in_dim.135
  168.9 0.1 copy.33
  169.0 0.1 broadcast_in_dim.136
  169.1 0.1 copy.32
  169.2 0.1 broadcast_in_dim.135
  169.3 0.1 copy.33
  169.4 0.1 broadcast_in_dim.136
  169.6 9.8 %all-gather.13.cloned.1.call-done = bf16[2048,512]{1,0:T(8,128)(2,1)} async-done(((bf16[512,512]{1,0:T(8,128)(2,1)}), bf16[2048,512]{1,0:T(8,128)(2,1)}) %all-gather.13.cloned.1.call-update) | async-done | bytes 2097168 | tf_op jit(solution)/shard_map/all_gather | solution.py:145
  179.5 2.2 convolution_convert_fusion.2
  181.7 11.4 %psum.7 = bf16[8,2048]{1,0:T(8,128)(2,1)S(1)} all-reduce(bf16[8,2048]{1,0:T(8,128)(2,1)S(1)} %convolution_convert_fusion.2), channel_id=1, replica_groups=mesh['grp'=2,'ctx'=4,'tp'=2,'sub'=2] {'tp','sub'}, use_global_device_ids=true, to_apply=%region_12.13 | all-reduce | flops 16384 | bytes 65536 | tf_op jit(solution)/shard_map/psum | solution.py:146
  193.1 0.1 fusion.28
  193.2 101.9 %all-gather.15.cloned.1.call-done = bf16[2048,3,512]{0,2,1:T(8,128)(2,1)} async-done(((bf16[512,3,512]{0,2,1:T(8,128)(2,1)}), bf16[2048,3,512]{0,2,1:T(8,128)(2,1)}) %all-gather.15.cloned.1.call-update) | async-done | bytes 6291472 | tf_op jit(solution)/shard_map/all_gather | solution.py:149
  295.2 4.5 %convolution_convert_fusion.1 = bf16[8,1536]{1,0:T(8,128)(2,1)S(1)} fusion(bf16[2048,1536]{0,1:T(8,128)(2,1)} %bitcast.115, bf16[8,2048]{1,0:T(8,128)(2,1)S(1)} %get-tuple-element.211, f32[2048]{0:T(1024)S(1)} %copy-done.6, f32[8]{0:T(128)S(1)} %add_rsqrt_fusion.1), kind=kOutput, calls=%fused_computation.17 | convolution fusion | flops 50409472 | bytes 6357024 | tf_op jit(solution)/shard_map/dot_general | solution.py:151
  299.7 13.6 %all_gather.45 = bf16[32,2,512]{2,0,1:T(8,128)(2,1)S(1)} all-gather(bf16[8,2,512]{2,0,1:T(8,128)(2,1)S(1)} %slice.143), channel_id=1, replica_groups=mesh['grp'=2,'ctx'=4,'tp'=2,'sub'=2] {'ctx'}, dimensions={0}, use_global_device_ids=true | all-gather | bytes 81920 | tf_op jit(solution)/shard_map/all_gather | solution.py:155
  313.3 0.2 fusion.143
  313.5 0.2 fusion.142
  313.8 0.2 fusion.141
  314.0 0.2 fusion.140
  314.2 0.2 fusion.92
  314.5 0.2 fusion.83
  314.7 0.2 fusion.80
  314.8 0.2 fusion.77
  315.0 0.2 fusion.74
  315.2 26.1 %all-gather.17.cloned.1.call-done = bf16[2048,512]{1,0:T(8,128)(2,1)} async-done(((bf16[512,512]{1,0:T(8,128)(2,1)}), bf16[2048,512]{1,0:T(8,128)(2,1)}) %all-gather.17.cloned.1.call-update) | async-done | bytes 2097168 | tf_op jit(solution)/shard_map/all_gather | solution.py:163
  341.3 2.9 convolution_convert_fusion
  344.2 18.3 %reduce-scatter.2.cloned.1.call-done = bf16[8,512]{1,0:T(8,128)(2,1)} async-done(((bf16[8,2048]{1,0:T(8,128)(2,1)}), bf16[8,512]{1,0:T(8,128)(2,1)}) %reduce-scatter.2.cloned.1.call-update) | async-done | bytes 8208 | tf_op jit(solution)/shard_map/reduce_scatter | solution.py:164
  362.5 1.3 add_convert_fusion
  (57 shorter events, 0.7 us)
Async XLA Ops:
  6.5 2.9 copy-start
  6.5 80.0 %all-gather.7.cloned.1.call-start = ((), (), s32[]{:S(2)}) async-start(), calls=%async_computation.1 | async-start | bytes 1966080 | tf_op jit(solution)/shard_map/all_gather | solution.py:118
  7.3 81.1 %all-gather.9.cloned.1.call-start = ((), (), s32[]{:S(2)}) async-start(), calls=%async_computation.2 | async-start | bytes 2621440 | tf_op jit(solution)/shard_map/all_gather | solution.py:126
  8.0 124.1 %all-gather.11.cloned.1.call-start = ((), (), s32[]{:S(2)}) async-start(), calls=%async_computation.3 | async-start | bytes 2621440 | tf_op jit(solution)/shard_map/all_gather | solution.py:131
  8.7 170.7 %all-gather.13.cloned.1.call-start = ((), (), s32[]{:S(2)}) async-start(), calls=%async_computation.4 | async-start | bytes 2621440 | tf_op jit(solution)/shard_map/all_gather | solution.py:145
  9.3 1.7 copy-start.2
  9.3 19.7 %copy-start.4 = (bf16[8,2048]{1,0:T(8,128)(2,1)S(1)}, bf16[8,2048]{1,0:T(8,128)(2,1)}, u32[]{:S(2)}) copy-start(bf16[8,2048]{1,0:T(8,128)(2,1)} %param.17) | copy-start | bytes 98308
  9.3 285.8 %all-gather.15.cloned.1.call-start = ((), (), s32[]{:S(2)}) async-start(), calls=%async_computation.5 | async-start | bytes 7864320 | tf_op jit(solution)/shard_map/all_gather | solution.py:149
  11.0 330.3 %all-gather.17.cloned.1.call-start = ((), (), s32[]{:S(2)}) async-start(), calls=%async_computation.6 | async-start | bytes 2621440 | tf_op jit(solution)/shard_map/all_gather | solution.py:163
  11.1 17.9 %collective-permute-start = (bf16[512,512]{1,0:T(8,128)(2,1)S(1)}, bf16[512,512]{1,0:T(8,128)(2,1)S(1)}, u32[]{:S(2)}, u32[]{:S(2)}) collective-permute-start(bf16[512,512]{1,0:T(8,128)(2,1)S(1)} %copy-done.2), channel_id=1, source_target_pairs={{0,4},{4,8},{8,12},{12,0},{1,5},{5,9},{9,13},{13,1},{2,6},{6,10},{... | collective-permute-start | bytes 1572872 | tf_op jit(solution)/shard_map/ppermute | solution.py:25
  14.1 24.8 %collective-permute-start.2 = (bf16[512,512]{1,0:T(8,128)(2,1)S(1)}, bf16[512,512]{1,0:T(8,128)(2,1)S(1)}, u32[]{:S(2)}, u32[]{:S(2)}) collective-permute-start(bf16[512,512]{1,0:T(8,128)(2,1)S(1)} %copy-done.2), channel_id=1, source_target_pairs={{4,0},{8,4},{12,8},{0,12},{5,1},{9,5},{13,9},{1,13},{6,2},{10,6},{... | collective-permute-start | bytes 1572872 | tf_op jit(solution)/shard_map/ppermute | solution.py:27
  16.3 346.2 %reduce-scatter.2.cloned.1.call-start = ((), (), s32[]{:S(2)}) async-start(), calls=%async_computation.7 | async-start | bytes 40960 | tf_op jit(solution)/shard_map/reduce_scatter | solution.py:164
  29.0 29.4 %collective-permute-start.1 = (bf16[512,512]{1,0:T(8,128)(2,1)S(1)}, bf16[512,512]{1,0:T(8,128)(2,1)S(1)}, u32[]{:S(2)}, u32[]{:S(2)}) collective-permute-start(bf16[512,512]{1,0:T(8,128)(2,1)S(1)} %collective-permute-done), channel_id=1, source_target_pairs={{0,4},{4,8},{8,12},{12,0},{1,5},{5,9},{9,13},{13,1},{2,6},{6,10},{... | collective-permute-start | bytes 1572872 | tf_op jit(solution)/shard_map/ppermute | solution.py:25
  39.0 19.4 %copy-start.3 = (bf16[512,512]{1,0:T(8,128)(2,1)}, bf16[512,512]{1,0:T(8,128)(2,1)S(1)}, u32[]{:S(2)}) copy-start(bf16[512,512]{1,0:T(8,128)(2,1)S(1)} %collective-permute-done.2) | copy-start | bytes 1572868
  59.7 2.0 copy-start.5
  61.7 26.7 %copy-start.8 = (f32[2048]{0:T(1024)S(1)}, f32[2048]{0:T(1024)}, u32[]{:S(2)}) copy-start(f32[2048]{0:T(1024)} %param.19) | copy-start | bytes 24580
  88.4 3.3 copy-start.7
  88.4 43.7 %copy-start.1 = (bf16[384,2048]{1,0:T(8,128)(2,1)S(1)}, bf16[384,2048]{1,0:T(8,128)(2,1)}, u32[]{:S(2)}) copy-start(bf16[384,2048]{1,0:T(8,128)(2,1)} %all-gather.7.cloned.1.call-done) | copy-start | bytes 4718596
  168.2 127.0 %copy-start.6 = (f32[2048]{0:T(1024)S(1)}, f32[2048]{0:T(1024)}, u32[]{:S(2)}) copy-start(f32[2048]{0:T(1024)} %param.21) | copy-start | bytes 24580
Sparse Core Ops, SparseCore 0:
  8.9 22.3 all-gather.6
  32.9 52.4 all-gather.8
  86.9 45.1 all-gather.10
  133.5 45.9 all-gather.12
  180.9 114.2 all-gather.14
  296.6 44.6 all-gather.16
  344.3 18.1 reduce-scatter.1
